TPU v7x, 256 devices: a whole 4x4x8 slice. The times are simulated.
256 devices in a mesh: pair: 64 (over z, x, y_lo), mo: 4 (over y_hi, core).
Axes of the slice: x: 4, y: 4 (y_hi: 2, y_lo: 2; y = y_hi * 2 + y_lo), z: 8, core: 2. Of those that a mesh axis runs over, the one named last changes fastest.
Arguments:
- integrals: bfloat16 [1024, 1000, 1000], P('pair', 'mo'), may hold values from -6 to 6
- coeffs: bfloat16 [1000, 512], replicated, may hold values from -0.1875 to 0.1875
- mirror: int32 [1024], replicated, may hold values from 0 to 1023, as said below
Outputs:
- combined: float32 [1024, 512, 512], P(None, 'pair', 'mo')
Inputs may be any that keep to these rules, and one draw needn't show every extreme that they name: mirror pairs the rows: mirror[mirror[k]] = k and mirror[k] != k for every row k; a row and its mirror may lie on any devices.
All inputs are finite; a program needn't handle non-finite values.
Results may differ from a plain program's by a relative error of at most 0.0029.
Values may be sent and summed in bfloat16 or wider, within the bound.
A program may use at most 128 MiB of HBM per device.

v0:
```python
import jax
import jax.numpy as jnp
from jax import lax
from jax.sharding import PartitionSpec as P


def on_device(integrals, coeffs, mirror):
    quarter = jnp.einsum(
        "krs,sj->krj", integrals, coeffs, preferred_element_type=jnp.float32
    ).astype(jnp.bfloat16)
    arrived = lax.all_to_all(quarter, "mo", split_axis=2, concat_axis=1, tiled=True)
    half = jnp.einsum("ri,krj->kij", coeffs, arrived, preferred_element_type=jnp.float32)
    pieces = lax.all_to_all(half, "pair", split_axis=1, concat_axis=0, tiled=True)
    partner = jnp.take(pieces, mirror, axis=0)
    return 0.5 * (pieces + partner)


def solution(mesh):
    return jax.shard_map(
        on_device,
        mesh=mesh,
        in_specs=(P("pair", "mo", None), P(), P()),
        out_specs=P(None, "pair", "mo"),
        check_vma=False,
    )
```

profile of v0, /device:TPU:2, one launch (start us, length us, event | category | flops | bytes accessed | tf_op | source)
XLA Modules:
  0.0 241.2 jit_solution(5012048735916774514)
XLA Ops:
  0.0 0.0 copy-start
  0.0 1.2 copy-done
  1.2 23.2 %fusion.4 = bf16[16,250,512]{2,1,0:T(8,128)(2,1)} fusion(bf16[16,250,1000]{2,0,1:T(8,128)(2,1)} %param.3, bf16[1000,512]{1,0:T(8,128)(2,1)S(1)} %copy-done), kind=kOutput, calls=%fused_computation.6 | convolution fusion | flops 4098048000 | bytes 13120000 | tf_op jit(solution)/shard_map/krs,sj->krj/dot_general | solution.py:8
  24.4 7.9 %copy.14 = bf16[16,250,512]{1,0,2:T(8,128)(2,1)} copy(bf16[16,250,512]{2,1,0:T(8,128)(2,1)} %fusion.4) | data formatting | bytes 8192000 | tf_op jit(solution)/shard_map/convert_element_type | solution.py:10
  32.3 55.3 %all_to_all.36 = bf16[16,250,512]{1,0,2:T(8,128)(2,1)} all-to-all(bf16[16,250,512]{1,0,2:T(8,128)(2,1)} %copy.14), channel_id=1, replica_groups=mesh['pair'=64,'mo'=4] {'mo'}, dimensions={2} | all-to-all | bytes 8192000 | tf_op jit(solution)/shard_map/all_to_all | solution.py:11
  87.7 8.5 %copy.16 = bf16[16,4,250,128]{3,0,2,1:T(8,128)(2,1)} copy(bf16[16,4,250,128]{2,0,3,1:T(8,128)(2,1)} %bitcast.18) | data formatting | bytes 8192000 | tf_op jit(solution)/shard_map/all_to_all | solution.py:11
  96.2 6.8 %fusion.7 = f32[16,512,128]{1,2,0:T(8,128)} fusion(bf16[16,1000,128]{2,0,1:T(8,128)(2,1)} %bitcast.17, bf16[1000,512]{1,0:T(8,128)(2,1)S(1)} %copy-done), kind=kOutput, calls=%fused_computation.7 | convolution fusion | flops 2097152000 | bytes 9314304 | tf_op jit(solution)/shard_map/ri,krj->kij/dot_general | solution.py:12
  103.1 5.5 %copy.18 = f32[16,512,128]{2,0,1:T(8,128)} copy(f32[16,512,128]{1,2,0:T(8,128)} %fusion.7) | data formatting | bytes 8388608 | tf_op jit(solution)/shard_map/ri,krj->kij/transpose | solution.py:12
  108.5 0.0 copy-start.1
  108.5 13.3 %all-to-all-start.1 = ((f32[16,512,128]{2,0,1:T(8,128)}), f32[16,512,128]{2,0,1:T(8,128)}, u32[]{:S(2)}, u32[]{:S(2)}) async-start(f32[16,512,128]{2,0,1:T(8,128)} %copy.18), calls=%async_computation.1 | async-start | bytes 8388608 | tf_op jit(solution)/shard_map/all_to_all | solution.py:13
  121.9 0.0 copy-done.1
  121.9 94.8 %all-to-all-done.1 = f32[16,512,128]{2,0,1:T(8,128)} async-done(((f32[16,512,128]{2,0,1:T(8,128)}), f32[16,512,128]{2,0,1:T(8,128)}, u32[]{:S(2)}, u32[]{:S(2)}) %all-to-all-start.1) | async-done | bytes 4194336 | tf_op jit(solution)/shard_map/all_to_all | solution.py:13
  216.8 6.1 %copy.20 = f32[64,16,8,128]{3,2,1,0:T(8,128)} copy(f32[64,16,8,128]{3,1,2,0:T(8,128)} %bitcast.8) | data formatting | bytes 8388608 | tf_op jit(solution)/shard_map/all_to_all | solution.py:13
  222.9 10.2 %gather_fusion = f32[1024,8,128]{2,1,0:T(8,128)} fusion(f32[1024,8,128]{2,1,0:T(8,128)} %bitcast.16, s32[1024]{0:T(1024)S(1)} %fusion.12), kind=kCustom, calls=%fused_computation | custom fusion | bytes 8392704 | tf_op jit(solution)/shard_map/jit(_take)/gather | solution.py:14
  233.1 8.1 %add_multiply_fusion = f32[1024,8,128]{2,1,0:T(8,128)} fusion(f32[1024,8,128]{2,1,0:T(8,128)} %gather_fusion, pred[1024]{0:T(1024)(128)(4,1)S(1)} %compare_and_fusion, f32[64,16,8,128]{3,2,1,0:T(8,128)} %copy.20), kind=kLoop, calls=%fused_computation.3 | loop fusion | flops 3145728 | bytes 12583936 | tf_op jit(solution)/shard_map/mul | solution.py:15
  (2 shorter events, 0.0 us)
Async XLA Ops:
  0.0 1.2 copy-start
  108.5 13.4 %copy-start.1 = (s32[1024]{0:T(1024)S(1)}, s32[1024]{0:T(1024)}, u32[]{:S(2)}) copy-start(s32[1024]{0:T(1024)} %param.5) | copy-start | bytes 12292
  108.5 108.2 %all-to-all-start.1 = ((f32[16,512,128]{2,0,1:T(8,128)}), f32[16,512,128]{2,0,1:T(8,128)}, u32[]{:S(2)}, u32[]{:S(2)}) async-start(f32[16,512,128]{2,0,1:T(8,128)} %copy.18), calls=%async_computation.1 | async-start | bytes 8388608 | tf_op jit(solution)/shard_map/all_to_all | solution.py:13
where the time goes:
time: 242 us; the launch traced here: 241 us
  waiting for transfers between devices  94.8 us (39%)
  blocking collectives  55.3 us (23%)
  local copies, waits for them, and re-layouts  39.5 us (16%)
  matrix products  30.1 us (12%)
  starting transfers between devices  13.3 us (5%)
  other arithmetic  8.1 us (3%)
    all_to_all x1, waiting for transfers between devices, on_device(): lax.all_to_all(half, 'pair', split_axis=1, concat_axis=0, tiled=True)  94.8 us
    all_to_all x1, blocking collectives, on_device(): lax.all_to_all(quarter, 'mo', split_axis=2, concat_axis=1, tiled=True)  55.3 us
    dot_general x1, matrix products, on_device(): jnp.einsum('krs,sj->krj', integrals, coeffs, preferred_element_type=jnp.f...  23.2 us
    all_to_all x1, starting transfers between devices, on_device(): lax.all_to_all(half, 'pair', split_axis=1, concat_axis=0, tiled=True)  13.3 us
    gather x1, local copies, waits for them, and re-layouts, on_device(): partner = jnp.take(pieces, mirror, axis=0)  10.2 us
    all_to_all x1, local copies, waits for them, and re-layouts, on_device(): lax.all_to_all(quarter, 'mo', split_axis=2, concat_axis=1, tiled=True)  8.54 us
    mul x1, other arithmetic, on_device(): return 0.5 * (pieces + partner)  8.09 us
    convert_element_type x1, local copies, waits for them, and re-layouts, on_device(): quarter = jnp.einsum('krs,sj->krj', integrals, coeffs, preferred_element_...  7.91 us
  transfers between devices with their start and end apart: 1, of which 1 were waited for; matrix products, arithmetic and copies ran while one was open for 0% of the time, Pallas kernels for 0%

commit v1 on v0

--- a/solution.py
+++ b/solution.py
@@ -5,10 +5,19 @@
 
 
 def on_device(integrals, coeffs, mirror):
+
+    def point_squares(body):
+        z1 = lax.psum(1, "mo")
+        y1 = jnp.split(body, z1, axis=2)
+        block_out = jnp.stack(y1)
+        moved = lax.all_to_all(block_out, "mo", 0, 0)
+        v1 = jnp.concatenate(moved, axis=1)
+        return v1
+
     quarter = jnp.einsum(
         "krs,sj->krj", integrals, coeffs, preferred_element_type=jnp.float32
     ).astype(jnp.bfloat16)
-    arrived = lax.all_to_all(quarter, "mo", split_axis=2, concat_axis=1, tiled=True)
+    arrived = point_squares(quarter)
     half = jnp.einsum("ri,krj->kij", coeffs, arrived, preferred_element_type=jnp.float32)
     pieces = lax.all_to_all(half, "pair", split_axis=1, concat_axis=0, tiled=True)
     partner = jnp.take(pieces, mirror, axis=0)

time: 242 us -> 223 us (0.921)
  local copies, waits for them, and re-layouts: 39.5 us -> 26.4 us
  matrix products: 30.1 us -> 26.6 us
    all_to_all x1 -> x0, local copies, waits for them, and re-layouts: 8.54 us -> none  [on_device(): lax.all_to_all(quarter, 'mo', split_axis=2, concat_axis=1, tiled=True)]
    convert_element_type x1 -> x0, local copies, waits for them, and re-layouts: 7.91 us -> none  [on_device(): quarter = jnp.einsum('krs,sj->krj', integrals, coeffs, preferred_element_...]
    another operation x0 -> x2, local copies, waits for them, and re-layouts: none -> 3.36 us  [point_squares(): block_out = jnp.stack(y1)]
    all_to_all x1, blocking collectives: 55.3 us -> 52.9 us  [point_squares(): moved = lax.all_to_all(block_out, 'mo', 0, 0)]
where the time goes in v1:
time: 223 us
  waiting for transfers between devices  95.3 us (43%)
  blocking collectives  52.9 us (24%)
  matrix products  26.6 us (12%)
  local copies, waits for them, and re-layouts  26.4 us (12%)
  starting transfers between devices  12.5 us (6%)
  other arithmetic  8.87 us (4%)
    all_to_all x1, waiting for transfers between devices, on_device(): lax.all_to_all(half, 'pair', split_axis=1, concat_axis=0, tiled=True)  95.3 us
    all_to_all x1, blocking collectives, point_squares(): moved = lax.all_to_all(block_out, 'mo', 0, 0)  52.9 us
    dot_general x1, matrix products, on_device(): jnp.einsum('krs,sj->krj', integrals, coeffs, preferred_element_type=jnp.f...  21.9 us
    all_to_all x1, starting transfers between devices, on_device(): lax.all_to_all(half, 'pair', split_axis=1, concat_axis=0, tiled=True)  12.5 us
    gather x1, local copies, waits for them, and re-layouts, on_device(): partner = jnp.take(pieces, mirror, axis=0)  10.2 us
    mul x1, other arithmetic, on_device(): return 0.5 * (pieces + partner)  8.09 us
    all_to_all x1, local copies, waits for them, and re-layouts, on_device(): lax.all_to_all(half, 'pair', split_axis=1, concat_axis=0, tiled=True)  6.1 us
    transpose x1, local copies, waits for them, and re-layouts, on_device(): jnp.einsum('ri,krj->kij', coeffs, arrived, preferred_element_type=jnp.flo...  5.45 us
  transfers between devices with their start and end apart: 1, of which 1 were waited for; matrix products, arithmetic and copies ran while one was open for 0% of the time, Pallas kernels for 0%

profile of v1, /device:TPU:2, one launch (start us, length us, event | category | flops | bytes accessed | tf_op | source)
XLA Modules:
  0.0 222.5 jit_solution(9054487274622792626)
XLA Ops:
  0.0 0.0 copy-start
  0.0 1.2 copy-done
  1.2 21.9 %fusion.4 = bf16[16,250,512]{2,1,0:T(8,128)(2,1)S(1)} fusion(bf16[16,250,1000]{2,0,1:T(8,128)(2,1)} %param.3, bf16[1000,512]{1,0:T(8,128)(2,1)S(1)} %copy-done), kind=kOutput, calls=%fused_computation.7 | convolution fusion | flops 4098048000 | bytes 13120000 | tf_op jit(solution)/shard_map/krs,sj->krj/dot_general | solution.py:17
  23.1 0.7 slice_bitcast_fusion.3
  23.8 0.8 pad_maximum_fusion
  24.6 2.6 %copy.12 = bf16[4,16,250,128]{3,1,2,0:T(8,128)(2,1)S(1)} copy(bf16[4,16,250,128]{3,2,1,0:T(8,128)(2,1)S(1)} %pad_maximum_fusion) | data formatting | bytes 8192000 | tf_op jit(solution)/shard_map/stack | solution.py:12
  27.3 52.9 %all_to_all.23 = bf16[4,16,250,128]{3,1,2,0:T(8,128)(2,1)S(1)} all-to-all(bf16[4,16,250,128]{3,1,2,0:T(8,128)(2,1)S(1)} %copy.12), channel_id=1, replica_groups=mesh['pair'=64,'mo'=4] {'mo'}, dimensions={0} | all-to-all | bytes 8192000 | tf_op jit(solution)/shard_map/all_to_all | solution.py:13
  80.1 4.7 %fusion.7 = f32[16,512,128]{1,2,0:T(8,128)} fusion(bf16[16,1000,128]{2,0,1:T(8,128)(2,1)S(1)} %bitcast.24, bf16[1000,512]{1,0:T(8,128)(2,1)S(1)} %copy-done), kind=kOutput, calls=%fused_computation.8 | convolution fusion | flops 2097152000 | bytes 9314304 | tf_op jit(solution)/shard_map/ri,krj->kij/dot_general | solution.py:21
  84.8 5.5 %copy.14 = f32[16,512,128]{2,0,1:T(8,128)} copy(f32[16,512,128]{1,2,0:T(8,128)} %fusion.7) | data formatting | bytes 8388608 | tf_op jit(solution)/shard_map/ri,krj->kij/transpose | solution.py:21
  90.3 0.0 copy-start.1
  90.3 12.5 %all-to-all-start.1 = ((f32[16,512,128]{2,0,1:T(8,128)}), f32[16,512,128]{2,0,1:T(8,128)}, u32[]{:S(2)}, u32[]{:S(2)}) async-start(f32[16,512,128]{2,0,1:T(8,128)} %copy.14), calls=%async_computation.1 | async-start | bytes 8388608 | tf_op jit(solution)/shard_map/all_to_all | solution.py:22
  102.7 0.0 copy-done.1
  102.8 95.3 %all-to-all-done.1 = f32[16,512,128]{2,0,1:T(8,128)} async-done(((f32[16,512,128]{2,0,1:T(8,128)}), f32[16,512,128]{2,0,1:T(8,128)}, u32[]{:S(2)}, u32[]{:S(2)}) %all-to-all-start.1) | async-done | bytes 4194336 | tf_op jit(solution)/shard_map/all_to_all | solution.py:22
  198.1 6.1 %copy.16 = f32[64,16,8,128]{3,2,1,0:T(8,128)} copy(f32[64,16,8,128]{3,1,2,0:T(8,128)} %bitcast.10) | data formatting | bytes 8388608 | tf_op jit(solution)/shard_map/all_to_all | solution.py:22
  204.2 10.2 %gather_fusion = f32[1024,8,128]{2,1,0:T(8,128)} fusion(f32[1024,8,128]{2,1,0:T(8,128)} %bitcast.23, s32[1024]{0:T(1024)S(1)} %fusion.12), kind=kCustom, calls=%fused_computation | custom fusion | bytes 8392704 | tf_op jit(solution)/shard_map/jit(_take)/gather | solution.py:23
  214.4 8.1 %add_multiply_fusion = f32[1024,8,128]{2,1,0:T(8,128)} fusion(f32[1024,8,128]{2,1,0:T(8,128)} %gather_fusion, pred[1024]{0:T(1024)(128)(4,1)S(1)} %compare_and_fusion, f32[64,16,8,128]{3,2,1,0:T(8,128)} %copy.16), kind=kLoop, calls=%fused_computation.4 | loop fusion | flops 3145728 | bytes 12583936 | tf_op jit(solution)/shard_map/mul | solution.py:24
  (2 shorter events, 0.0 us)
Async XLA Ops:
  0.0 1.2 copy-start
  90.3 12.5 %copy-start.1 = (s32[1024]{0:T(1024)S(1)}, s32[1024]{0:T(1024)}, u32[]{:S(2)}) copy-start(s32[1024]{0:T(1024)} %param.5) | copy-start | bytes 12292
  90.3 107.8 %all-to-all-start.1 = ((f32[16,512,128]{2,0,1:T(8,128)}), f32[16,512,128]{2,0,1:T(8,128)}, u32[]{:S(2)}, u32[]{:S(2)}) async-start(f32[16,512,128]{2,0,1:T(8,128)} %copy.14), calls=%async_computation.1 | async-start | bytes 8388608 | tf_op jit(solution)/shard_map/all_to_all | solution.py:22
